TPU v7x, 32 devices: a whole 2x2x4 slice. The times are simulated.
32 devices in a mesh: dp: 8 (over z, x), th: 2 (over core), tw: 2 (over y).
Axes of the slice: x: 2, y: 2, z: 4, core: 2. Of those that a mesh axis runs over, the one named last changes fastest.
Arguments:
- tokens: bfloat16 [16, 1536, 768], P('dp', ('th', 'tw')), may hold values from -6 to 6
- segment_ids: int32 [16, 1536], P('dp'), may hold values from 0 to 7, never falling along the last dimension, each value on 1 to 768 neighbouring positions
- norm1_gain: float32 [768], replicated, may hold values from 0.5 to 1.5
- norm1_shift: float32 [768], replicated, may hold values from -3 to 3
- w_qkv: bfloat16 [3, 768, 768], P(None, None, ('th', 'tw')), may hold values from -0.21875 to 0.21875
- b_qv: float32 [2, 768], P(None, ('th', 'tw')), may hold values from -3 to 3
- w_out: bfloat16 [768, 768], P(('th', 'tw')), may hold values from -0.875 to 0.875
- b_out: float32 [768], replicated, may hold values from -3 to 3
- norm2_gain: float32 [768], replicated, may hold values from 0.5 to 1.5
- norm2_shift: float32 [768], replicated, may hold values from -3 to 3
- w_up: bfloat16 [768, 3072], replicated, may hold values from -0.21875 to 0.21875
- b_up: float32 [3072], replicated, may hold values from -3 to 3
- w_down: bfloat16 [3072, 768], replicated, may hold values from -0.109375 to 0.109375
- b_down: float32 [768], replicated, may hold values from -3 to 3
- cotangent: bfloat16 [16, 1536, 768], P('dp', ('th', 'tw')), may hold values from -6 to 6
Outputs:
- block_out: bfloat16 [16, 1536, 768], P('dp', ('th', 'tw'))
- grad_tokens: bfloat16 [16, 1536, 768], P('dp', ('th', 'tw'))
- grad_norm1_gain: float32 [768], replicated
- grad_norm1_shift: float32 [768], replicated
- grad_w_qkv: float32 [3, 768, 768], P(None, None, ('th', 'tw'))
- grad_b_qv: float32 [2, 768], P(None, ('th', 'tw'))
- grad_w_out: float32 [768, 768], P(('th', 'tw'))
- grad_b_out: float32 [768], replicated
- grad_norm2_gain: float32 [768], replicated
- grad_norm2_shift: float32 [768], replicated
- grad_w_up: float32 [768, 3072], replicated
- grad_b_up: float32 [3072], replicated
- grad_w_down: float32 [3072, 768], replicated
- grad_b_down: float32 [768], replicated
Inputs may be any that keep to these rules, and one draw needn't show every extreme that they name: `segment_ids`: within each row the ids never fall, and one image holds 1 to 768 tokens.
All inputs are finite; a program needn't handle non-finite values.
Results may differ from a plain program's by a relative error of at most 0.015.
Values may be sent and summed in bfloat16 or wider, within the bound.
A program may use at most 192 MiB of HBM per device.

v0:
```python
import jax
import jax.numpy as jnp
from jax import lax
from jax.sharding import PartitionSpec as P

HD = 64
EPSILON = 1e-06


def layer_norm(field, norm_gain, norm_shift):
    average = jnp.mean(field, axis=-1, keepdims=True)
    centred = field - average
    spread = jnp.mean(centred * centred, axis=-1, keepdims=True)
    return centred * lax.rsqrt(spread + EPSILON) * norm_gain + norm_shift


def gelu_exact(field):
    return jax.nn.gelu(field, approximate=False)


def masked_scores(query_block, key_rows, row_seg, offset, block_rows):
    score_scale = query_block.shape[-1] ** (-0.5)
    same_image = row_seg[offset : offset + block_rows, None] == row_seg[None, :]
    scores = (
        jnp.einsum("qhe,khe->hqk", query_block, key_rows, preferred_element_type=jnp.float32)
        * score_scale
    )
    return jnp.where(same_image[None], scores, -1000000000.0)


def row_forward(row_items):
    row_qkv, row_seg = row_items
    length = row_qkv.shape[1]
    head_count = row_qkv.shape[2] // HD
    key_rows = row_qkv[1].reshape(length, head_count, HD)
    value_rows = row_qkv[2].reshape(length, head_count, HD)
    block_rows = min(512, length)
    head_outs = []
    log_totals = []
    for offset in range(0, length, block_rows):
        query_block = row_qkv[0, offset : offset + block_rows].reshape(block_rows, head_count, HD)
        scores = masked_scores(query_block, key_rows, row_seg, offset, block_rows)
        row_peak = jnp.max(scores, axis=-1, keepdims=True)
        exponent = jnp.exp(scores - row_peak)
        denominator = jnp.sum(exponent, axis=-1, keepdims=True)
        weights_low = (exponent / denominator).astype(jnp.bfloat16)
        head_out = jnp.einsum(
            "hqk,khe->qhe", weights_low, value_rows, preferred_element_type=jnp.float32
        )
        head_outs.append(head_out.reshape(block_rows, head_count * HD).astype(jnp.bfloat16))
        log_totals.append((row_peak + jnp.log(denominator))[..., 0])
    return (jnp.concatenate(head_outs, 0), jnp.concatenate(log_totals, 1))


def row_backward(row_items):
    row_qkv, row_grad, row_total, row_seg = row_items
    length = row_qkv.shape[1]
    head_count = row_qkv.shape[2] // HD
    score_scale = HD ** (-0.5)
    key_rows = row_qkv[1].reshape(length, head_count, HD)
    value_rows = row_qkv[2].reshape(length, head_count, HD)
    block_rows = min(512, length)
    key_grad = jnp.zeros((length, head_count, HD), jnp.float32)
    value_grad = jnp.zeros((length, head_count, HD), jnp.float32)
    query_grads = []
    for offset in range(0, length, block_rows):
        query_block = row_qkv[0, offset : offset + block_rows].reshape(block_rows, head_count, HD)
        upstream = row_grad[offset : offset + block_rows].reshape(block_rows, head_count, HD)
        scores = masked_scores(query_block, key_rows, row_seg, offset, block_rows)
        probability = jnp.exp(scores - row_total[:, offset : offset + block_rows, None])
        value_grad = value_grad + jnp.einsum(
            "hqk,qhe->khe",
            probability.astype(jnp.bfloat16),
            upstream,
            preferred_element_type=jnp.float32,
        )
        prob_grad = jnp.einsum(
            "qhe,khe->hqk", upstream, value_rows, preferred_element_type=jnp.float32
        )
        row_inner = jnp.sum(probability * prob_grad, axis=-1, keepdims=True)
        score_grad = (probability * (prob_grad - row_inner)).astype(jnp.bfloat16) * score_scale
        query_grad = jnp.einsum(
            "hqk,khe->qhe", score_grad, key_rows, preferred_element_type=jnp.float32
        )
        query_grads.append(query_grad.reshape(block_rows, head_count * HD))
        key_grad = key_grad + jnp.einsum(
            "hqk,qhe->khe", score_grad, query_block, preferred_element_type=jnp.float32
        )
    stacked = jnp.stack(
        [
            jnp.concatenate(query_grads, 0),
            key_grad.reshape(length, head_count * HD),
            value_grad.reshape(length, head_count * HD),
        ]
    )
    return stacked.astype(jnp.bfloat16)


def body(
    tokens,
    segment_ids,
    norm1_gain,
    norm1_shift,
    w_qkv,
    b_qv,
    w_out,
    b_out,
    norm2_gain,
    norm2_shift,
    w_up,
    b_up,
    w_down,
    b_down,
    cotangent,
):
    inputs = tokens.astype(jnp.float32)
    normed_one, norm_one_back = jax.vjp(layer_norm, inputs, norm1_gain, norm1_shift)
    normed_low = normed_one.astype(jnp.bfloat16)
    gathered = lax.all_gather(normed_low, ("th", "tw"), axis=1, tiled=True)
    bias_rows = jnp.stack([b_qv[0], jnp.zeros_like(b_qv[0]), b_qv[1]])
    projected = jnp.einsum("rld,cde->rcle", gathered, w_qkv, preferred_element_type=jnp.float32)
    projected_low = (projected + bias_rows[None, :, None, :]).astype(jnp.bfloat16)
    heads_out, totals = lax.map(row_forward, (projected_low, segment_ids))
    partial_out = jnp.einsum("rle,ed->rld", heads_out, w_out, preferred_element_type=jnp.float32)
    branch = (
        lax.psum_scatter(
            partial_out.astype(jnp.bfloat16), ("th", "tw"), scatter_dimension=1, tiled=True
        ).astype(jnp.float32)
        + b_out
    )
    middle = inputs + branch
    normed_two, norm_two_back = jax.vjp(layer_norm, middle, norm2_gain, norm2_shift)
    second_low = normed_two.astype(jnp.bfloat16)
    hidden_pre = (
        jnp.einsum("rld,df->rlf", second_low, w_up, preferred_element_type=jnp.float32) + b_up
    )
    activated, gelu_back = jax.vjp(gelu_exact, hidden_pre)
    active_low = activated.astype(jnp.bfloat16)
    block_out = middle + (
        jnp.einsum("rlf,fd->rld", active_low, w_down, preferred_element_type=jnp.float32) + b_down
    )
    upstream = cotangent.astype(jnp.float32)
    grad_w_down = jnp.einsum(
        "rlf,rld->fd", active_low, cotangent, preferred_element_type=jnp.float32
    )
    grad_b_down = jnp.sum(upstream, axis=(0, 1))
    grad_active = jnp.einsum("rld,fd->rlf", cotangent, w_down, preferred_element_type=jnp.float32)
    grad_hidden = gelu_back(grad_active)[0].astype(jnp.bfloat16)
    grad_w_up = jnp.einsum(
        "rld,rlf->df", second_low, grad_hidden, preferred_element_type=jnp.float32
    )
    grad_b_up = jnp.sum(grad_hidden.astype(jnp.float32), axis=(0, 1))
    grad_normed_two = jnp.einsum(
        "rlf,df->rld", grad_hidden, w_up, preferred_element_type=jnp.float32
    )
    grad_mid_norm, grad_gain_two, grad_shift_two = norm_two_back(grad_normed_two)
    grad_middle = upstream + grad_mid_norm
    grad_branch = grad_middle.astype(jnp.bfloat16)
    grad_b_out = jnp.sum(grad_branch.astype(jnp.float32), axis=(0, 1))
    grad_whole = lax.all_gather(grad_branch, ("th", "tw"), axis=1, tiled=True)
    grad_heads = jnp.einsum(
        "rld,ed->rle", grad_whole, w_out, preferred_element_type=jnp.float32
    ).astype(jnp.bfloat16)
    grad_w_out = jnp.einsum(
        "rle,rld->ed", heads_out, grad_whole, preferred_element_type=jnp.float32
    )
    grad_qkv = lax.map(row_backward, (projected_low, grad_heads, totals, segment_ids))
    grad_w_qkv = jnp.einsum("rld,rcle->cde", gathered, grad_qkv, preferred_element_type=jnp.float32)
    grad_b_qv = jnp.sum(grad_qkv[:, 0::2].astype(jnp.float32), axis=(0, 2))
    grad_normed = jnp.einsum("rcle,cde->rld", grad_qkv, w_qkv, preferred_element_type=jnp.float32)
    grad_tile = lax.psum_scatter(
        grad_normed.astype(jnp.bfloat16), ("th", "tw"), scatter_dimension=1, tiled=True
    ).astype(jnp.float32)
    grad_inputs, grad_gain_one, grad_shift_one = norm_one_back(grad_tile)
    grad_tokens = (grad_middle + grad_inputs).astype(jnp.bfloat16)
    head_sums = (
        lax.psum(grad_w_qkv.astype(jnp.bfloat16), "dp").astype(jnp.float32),
        lax.psum(grad_b_qv.astype(jnp.bfloat16), "dp").astype(jnp.float32),
        lax.psum(grad_w_out.astype(jnp.bfloat16), "dp").astype(jnp.float32),
    )
    shared = lax.psum(
        (
            grad_gain_one,
            grad_shift_one,
            grad_b_out,
            grad_gain_two,
            grad_shift_two,
            grad_w_up,
            grad_b_up,
            grad_w_down,
            grad_b_down,
        ),
        ("dp", "th", "tw"),
    )
    return (
        block_out.astype(jnp.bfloat16),
        grad_tokens,
        shared[0],
        shared[1],
        head_sums[0],
        head_sums[1],
        head_sums[2],
        shared[2],
        shared[3],
        shared[4],
        shared[5],
        shared[6],
        shared[7],
        shared[8],
    )


def solution(mesh):
    return jax.shard_map(
        body,
        mesh=mesh,
        in_specs=(
            P("dp", ("th", "tw"), None),
            P("dp", None),
            P(),
            P(),
            P(None, None, ("th", "tw")),
            P(None, ("th", "tw")),
            P(("th", "tw"), None),
            P(),
            P(),
            P(),
            P(),
            P(),
            P(),
            P(),
            P("dp", ("th", "tw"), None),
        ),
        out_specs=(
            P("dp", ("th", "tw"), None),
            P("dp", ("th", "tw"), None),
            P(),
            P(),
            P(None, None, ("th", "tw")),
            P(None, ("th", "tw")),
            P(("th", "tw"), None),
            P(),
            P(),
            P(),
            P(),
            P(),
            P(),
            P(),
        ),
        check_vma=False,
    )
```

profile of v0, /device:TPU:0, one launch (start us, length us, event | category | flops | bytes accessed | tf_op | source)
XLA Modules:
  0.0 1006.1 jit_solution(13144696597506998621)
XLA Ops:
  14.8 40.1 %all-gather.3.cloned.1.call-done = bf16[2,1536,768]{2,1,0:T(8,128)(2,1)} async-done(((bf16[2,384,768]{2,1,0:T(8,128)(2,1)}), bf16[2,1536,768]{2,1,0:T(8,128)(2,1)}) %all-gather.3.cloned.1.call-update) | async-done | bytes 4718608 | tf_op jit(solution)/shard_map/all_gather | solution.py:119
  54.9 6.7 fusion.154
  61.6 59.3 %while.22 = (s32[]{:T(128)}, bf16[2,1536,192]{1,2,0:T(8,128)(2,1)S(1)}, f32[2,3,1536]{2,1,0:T(4,128)S(1)}, bf16[2,3,1536,192]{2,3,1,0:T(8,128)(2,1)}, s32[2,1536...) while((s32[]{:T(128)}, bf16[2,1536,192]{1,2,0:T(8,128)(2,1)S(1)}, ...), condition=%wide.region_9.10_spmd, body=%wide.region_2.9_spmd.sunk | while | flops 1901302272 | bytes 107581632 | solution.py:123
  78.7 5.2 fusion.324
  87.4 3.5 fusion.325
  108.0 5.2 fusion.324
  120.9 4.9 convolution_convert_fusion
  125.9 47.9 %reduce-scatter.3.cloned.1.call-done = bf16[2,384,768]{2,1,0:T(8,128)(2,1)} async-done(((bf16[2,1536,768]{2,1,0:T(8,128)(2,1)}), bf16[2,384,768]{2,1,0:T(8,128)(2,1)}) %reduce-scatter.3.cloned.1.call-update) | async-done | bytes 1179664 | tf_op jit(solution)/shard_map/reduce_scatter | solution.py:126
  177.7 9.2 fusion.165
  186.9 23.4 %multiply_convert_fusion.3 = (bf16[2,384,3072]{2,1,0:T(8,128)(2,1)}, f32[2,384,3072]{2,1,0:T(8,128)}) fusion(f32[2,384,3072]{2,1,0:T(8,128)S(1)} %get-tuple-element.164, f32[3072]{0:T(1024)S(1)} %copy-done.45, u8[384,3072]{1,0:T(8,128)(4,1)S(1)} %get-tuple-element.78, u8[384,3072]{1,0:T(8,128)(4,1)S(1)} %get-tuple-element.77), kind=kLoop, calls=%fused_computation.126 | loop fusion | flops 167510016 | bytes 25964544 | tf_op jit(solution)/shard_map/convert_element_type | solution.py:138
  210.2 12.5 %convert_reduce_fusion = (f32[3072]{0:T(1024)}, bf16[2,384,3072]{2,1,0:T(8,128)(2,1)}) fusion(f32[2,384,3072]{2,1,0:T(8,128)} %get-tuple-element.123, bf16[2,384,768]{2,1,0:T(8,128)(2,1)S(1)} %copy-done.15, bf16[3072,768]{1,0:T(8,128)(2,1)} %param.31, f32[2,384,3072]{2,1,0:T(8,128)S(1)} %get-tuple-element.164, f32[3072]{0:T(1024)S(1)} %copy-done.45), kind=kOutput, calls=%fused_computation.124 | convolution fusion | flops 3663983616 | bytes 29515776 | tf_op jit(solution)/shard_map/rld,fd->rlf/dot_general | solution.py:147
  222.8 8.1 fusion.185
  235.7 37.6 %all-gather.5.cloned.1.call-done = bf16[2,1536,768]{2,1,0:T(8,128)(2,1)} async-done(((bf16[2,384,768]{2,1,0:T(8,128)(2,1)}), bf16[2,1536,768]{2,1,0:T(8,128)(2,1)}) %all-gather.5.cloned.1.call-update) | async-done | bytes 4718608 | tf_op jit(solution)/shard_map/all_gather | solution.py:160
  273.3 5.0 convolution_convert_fusion.1
  278.3 254.2 %while.23 = (s32[]{:T(128)}, bf16[2,3,1536,192]{2,3,1,0:T(8,128)(2,1)}, bf16[2,3,1536,192]{2,3,1,0:T(8,128)(2,1)}, s32[2,1536]{1,0:T(2,128)S(1)}, f32[2,3,1536]{...) while((s32[]{:T(128)}, ...), condition=%wide.region_19.20_spmd, body=%wide.region_15.19_spmd.sunk | while | flops 4682926080 | bytes 364640672 | solution.py:167
  294.2 4.3 copy-done.3
  300.4 5.2 fusion.371
  305.6 15.2 %fusion.377 = bf16[3,64,512]{2,1,0:T(8,128)(2,1)} fusion(bf16[1536,3,64]{0,2,1:T(8,128)(2,1)S(1)} %bitcast.312, f32[3,512,1536]{2,1,0:T(8,128)} %copy-done.4, f32[3,512,1536]{2,1,0:T(8,128)} %fusion.371), kind=kOutput, calls=%fused_computation.94.clone.1 | convolution fusion | flops 320965632 | bytes 19660800 | tf_op jit(solution)/shard_map/while/body/eval_jaxpr/hqk,khe->qhe/dot_general | solution.py:82
  320.8 15.3 %fusion.372 = f32[3,64,1536]{2,1,0:T(8,128)} fusion(bf16[512,3,64]{0,2,1:T(8,128)(2,1)} %bitcast.323, f32[3,512,1536]{2,1,0:T(8,128)} %copy-done.4, f32[3,512,1536]{2,1,0:T(8,128)} %fusion.371), kind=kOutput, calls=%fused_computation.63.clone.1 | convolution fusion | flops 320867328 | bytes 20250624 | tf_op jit(solution)/shard_map/while/body/eval_jaxpr/hqk,qhe->khe/dot_general | solution.py:86
  336.1 5.2 fusion.375
  341.3 14.4 %fusion.379 = bf16[3,64,512]{2,1,0:T(8,128)(2,1)S(1)} fusion(bf16[1536,3,64]{0,2,1:T(8,128)(2,1)S(1)} %bitcast.313, f32[3,512,1536]{2,1,0:T(8,128)} %copy-done.3, f32[3,512,1536]{2,1,0:T(8,128)} %fusion.375), kind=kOutput, calls=%fused_computation.92.clone.1 | convolution fusion | flops 320965632 | bytes 19660800 | tf_op jit(solution)/shard_map/while/body/eval_jaxpr/hqk,khe->qhe/dot_general | solution.py:82
  355.6 5.2 fusion.373
  360.8 15.0 %fusion.378 = bf16[3,64,512]{2,1,0:T(8,128)(2,1)} fusion(bf16[1536,3,64]{0,2,1:T(8,128)(2,1)S(1)} %bitcast.314, f32[3,512,1536]{2,1,0:T(8,128)} %copy-done.2, f32[3,512,1536]{2,1,0:T(8,128)} %fusion.373), kind=kOutput, calls=%fused_computation.93.clone.1 | convolution fusion | flops 320965632 | bytes 19660800 | tf_op jit(solution)/shard_map/while/body/eval_jaxpr/hqk,khe->qhe/dot_general | solution.py:82
  375.8 14.1 %fusion.374 = f32[3,64,1536]{2,1,0:T(8,128)} fusion(bf16[512,3,64]{0,2,1:T(8,128)(2,1)S(1)} %bitcast.321, f32[3,512,1536]{2,1,0:T(8,128)} %copy-done.2, f32[3,512,1536]{2,1,0:T(8,128)} %fusion.373), kind=kOutput, calls=%fused_computation.67.clone.1 | convolution fusion | flops 320867328 | bytes 20250624 | tf_op jit(solution)/shard_map/while/body/eval_jaxpr/hqk,qhe->khe/dot_general | solution.py:86
  389.9 14.1 %fusion.376 = bf16[3,64,1536]{2,1,0:T(8,128)(2,1)S(1)} fusion(f32[3,64,1536]{2,1,0:T(8,128)} %fusion.372, f32[3,64,1536]{2,1,0:T(8,128)} %fusion.374, bf16[512,3,64]{0,2,1:T(8,128)(2,1)S(1)} %bitcast.319, f32[3,512,1536]{2,1,0:T(8,128)} %copy-done.3, f32[3,512,1536]{2,1,0:T(8,128)} %fusion.375), kind=kOutput, calls=%fused_computation.79.clone.1 | convolution fusion | flops 321752064 | bytes 22020096 | tf_op jit(solution)/shard_map/while/body/eval_jaxpr/hqk,qhe->khe/dot_general | solution.py:86
  421.0 4.3 copy-done.3
  427.2 5.2 fusion.371
  432.4 15.2 %fusion.377 = bf16[3,64,512]{2,1,0:T(8,128)(2,1)} fusion(bf16[1536,3,64]{0,2,1:T(8,128)(2,1)S(1)} %bitcast.312, f32[3,512,1536]{2,1,0:T(8,128)} %copy-done.4, f32[3,512,1536]{2,1,0:T(8,128)} %fusion.371), kind=kOutput, calls=%fused_computation.94.clone.1 | convolution fusion | flops 320965632 | bytes 19660800 | tf_op jit(solution)/shard_map/while/body/eval_jaxpr/hqk,khe->qhe/dot_general | solution.py:82
  447.6 15.3 %fusion.372 = f32[3,64,1536]{2,1,0:T(8,128)} fusion(bf16[512,3,64]{0,2,1:T(8,128)(2,1)} %bitcast.323, f32[3,512,1536]{2,1,0:T(8,128)} %copy-done.4, f32[3,512,1536]{2,1,0:T(8,128)} %fusion.371), kind=kOutput, calls=%fused_computation.63.clone.1 | convolution fusion | flops 320867328 | bytes 20250624 | tf_op jit(solution)/shard_map/while/body/eval_jaxpr/hqk,qhe->khe/dot_general | solution.py:86
  462.9 5.2 fusion.375
  468.1 14.4 %fusion.379 = bf16[3,64,512]{2,1,0:T(8,128)(2,1)S(1)} fusion(bf16[1536,3,64]{0,2,1:T(8,128)(2,1)S(1)} %bitcast.313, f32[3,512,1536]{2,1,0:T(8,128)} %copy-done.3, f32[3,512,1536]{2,1,0:T(8,128)} %fusion.375), kind=kOutput, calls=%fused_computation.92.clone.1 | convolution fusion | flops 320965632 | bytes 19660800 | tf_op jit(solution)/shard_map/while/body/eval_jaxpr/hqk,khe->qhe/dot_general | solution.py:82
  482.5 5.2 fusion.373
  487.6 15.0 %fusion.378 = bf16[3,64,512]{2,1,0:T(8,128)(2,1)} fusion(bf16[1536,3,64]{0,2,1:T(8,128)(2,1)S(1)} %bitcast.314, f32[3,512,1536]{2,1,0:T(8,128)} %copy-done.2, f32[3,512,1536]{2,1,0:T(8,128)} %fusion.373), kind=kOutput, calls=%fused_computation.93.clone.1 | convolution fusion | flops 320965632 | bytes 19660800 | tf_op jit(solution)/shard_map/while/body/eval_jaxpr/hqk,khe->qhe/dot_general | solution.py:82
  502.6 14.1 %fusion.374 = f32[3,64,1536]{2,1,0:T(8,128)} fusion(bf16[512,3,64]{0,2,1:T(8,128)(2,1)S(1)} %bitcast.321, f32[3,512,1536]{2,1,0:T(8,128)} %copy-done.2, f32[3,512,1536]{2,1,0:T(8,128)} %fusion.373), kind=kOutput, calls=%fused_computation.67.clone.1 | convolution fusion | flops 320867328 | bytes 20250624 | tf_op jit(solution)/shard_map/while/body/eval_jaxpr/hqk,qhe->khe/dot_general | solution.py:86
  516.8 14.1 %fusion.376 = bf16[3,64,1536]{2,1,0:T(8,128)(2,1)S(1)} fusion(f32[3,64,1536]{2,1,0:T(8,128)} %fusion.372, f32[3,64,1536]{2,1,0:T(8,128)} %fusion.374, bf16[512,3,64]{0,2,1:T(8,128)(2,1)S(1)} %bitcast.319, f32[3,512,1536]{2,1,0:T(8,128)} %copy-done.3, f32[3,512,1536]{2,1,0:T(8,128)} %fusion.375), kind=kOutput, calls=%fused_computation.79.clone.1 | convolution fusion | flops 321752064 | bytes 22020096 | tf_op jit(solution)/shard_map/while/body/eval_jaxpr/hqk,qhe->khe/dot_general | solution.py:86
  532.5 4.6 fusion.177
  537.2 6.2 fusion.174
  543.4 7.7 bitcast_convert_fusion
  551.2 10.5 %convolution_bitcast_fusion = f32[3072,768]{1,0:T(8,128)} fusion(bf16[2,384,3072]{2,1,0:T(8,128)(2,1)} %get-tuple-element.122, bf16[2,384,768]{2,1,0:T(8,128)(2,1)} %param.33), kind=kOutput, calls=%fused_computation.140 | convolution fusion | flops 3623878656 | bytes 15335424 | tf_op jit(solution)/shard_map/rlf,rld->fd/dot_general | solution.py:143
  561.7 9.2 convolution_bitcast_fusion.1
  571.7 8.8 add_convert_fusion.3
  580.9 21.5 %psum.87 = bf16[2,192]{1,0:T(2,128)(2,1)S(1)} all-reduce(bf16[2,192]{1,0:T(2,128)(2,1)S(1)} %slice_reduce_fusion), channel_id=1, replica_groups=mesh['dp'=8,'th'=2,'tw'=2] {'dp'}, use_global_device_ids=true, to_apply=%region_29.30 | all-reduce | flops 384 | bytes 1536 | tf_op jit(solution)/shard_map/psum | solution.py:178
  603.0 20.8 %all-reduce.8.cloned.1.call-done = (bf16[3,768,192]{1,2,0:T(8,128)(2,1)}, bf16[192,768]{1,0:T(8,128)(2,1)}) async-done(((bf16[3,768,192]{1,2,0:T(8,128)(2,1)}, bf16[192,768]{1,0:T(8,128)(2,1)}), (bf16[3,768,192]{1,2,0:T(8,128)(2,1)}, bf16[192,768]{1,0:T(8,128)(2,1)})) %all-reduce.8.cloned.1.call-update) | async-done | bytes 1179664 | tf_op jit(solution)/shard_map/psum | solution.py:177
  628.1 45.2 %reduce-scatter.5.cloned.1.call-done = bf16[2,384,768]{2,1,0:T(8,128)(2,1)} async-done(((bf16[2,1536,768]{2,1,0:T(8,128)(2,1)}), bf16[2,384,768]{2,1,0:T(8,128)(2,1)}) %reduce-scatter.5.cloned.1.call-update) | async-done | bytes 1179664 | tf_op jit(solution)/shard_map/reduce_scatter | solution.py:171
  681.4 42.5 %all-reduce = (f32[768]{0:T(1024)}, f32[768]{0:T(1024)}, f32[768]{0:T(1024)}, f32[768]{0:T(1024)}, f32[768]{0:T(1024)}, /*index=5*/f32[3072]{0:T(1024)}, f32[768]{0:T(1024)}) all-reduce(f32[768]{0:T(1024)S(1)} %get-tuple-element.81, f32[768]{0:T(1024)S(1)} %get-tuple-element.85, ...), channel_id=1, replica_groups=mesh['dp'=8,'th'=2,'tw'=2] {'dp','th','tw'}, use_global_device_ids=true, to_apply=%region_24.25 | all-reduce | flops 7680 | bytes 61440 | tf_op jit(solution)/shard_map/psum | solution.py:181
  724.0 262.5 %all-reduce.6.cloned.1.call-done = (f32[768,3072]{1,0:T(8,128)}, f32[3072,768]{1,0:T(8,128)}) async-done(((f32[768,3072]{1,0:T(8,128)}, f32[3072,768]{1,0:T(8,128)}), (f32[768,3072]{1,0:T(8,128)}, f32[3072,768]{1,0:T(8,128)})) %all-reduce.6.cloned.1.call-update) | async-done | bytes 18874384 | tf_op jit(solution)/shard_map/psum | solution.py:181
  986.5 8.8 copy.59
  995.2 3.7 copy.60
  (228 shorter events, 112.1 us)
Async XLA Ops:
  7.2 47.7 %copy-start = (bf16[3,768,192]{1,2,0:T(8,128)(2,1)S(1)}, bf16[3,768,192]{1,2,0:T(8,128)(2,1)}, u32[]{:S(2)}) copy-start(bf16[3,768,192]{1,2,0:T(8,128)(2,1)} %param.23) | copy-start | bytes 2654212
  7.2 7.5 copy-start.48
  7.2 47.7 %all-gather.3.cloned.1.call-start = ((), (), s32[]{:S(2)}) async-start(), calls=%async_computation.2 | async-start | bytes 5898240 | tf_op jit(solution)/shard_map/all_gather | solution.py:119
  14.6 159.3 %reduce-scatter.3.cloned.1.call-start = ((), (), s32[]{:S(2)}) async-start(), calls=%async_computation.3 | async-start | bytes 5898240 | tf_op jit(solution)/shard_map/reduce_scatter | solution.py:126
  14.8 46.8 %copy-start.20 = (s32[2,1536]{1,0:T(2,128)S(1)}, s32[2,1536]{1,0:T(2,128)}, u32[]{:S(2)}) copy-start(s32[2,1536]{1,0:T(2,128)} %param.20) | copy-start | bytes 36868
  120.8 5.0 copy-start.17
  120.9 53.0 %copy-start.5 = (bf16[2,384,768]{2,1,0:T(8,128)(2,1)S(1)}, bf16[2,384,768]{2,1,0:T(8,128)(2,1)}, u32[]{:S(2)}) copy-start(bf16[2,384,768]{2,1,0:T(8,128)(2,1)} %param.19) | copy-start | bytes 3538948
  120.9 53.0 %copy-start.21 = (f32[768]{0:T(1024)S(1)}, f32[768]{0:T(1024)}, u32[]{:S(2)}) copy-start(f32[768]{0:T(1024)} %param.26) | copy-start | bytes 9220
  125.8 51.8 %copy-start.25 = (f32[768]{0:T(1024)S(1)}, f32[768]{0:T(1024)}, u32[]{:S(2)}) copy-start(f32[768]{0:T(1024)} %param.27) | copy-start | bytes 9220
  125.8 51.8 %copy-start.30 = (f32[768]{0:T(1024)S(1)}, f32[768]{0:T(1024)}, u32[]{:S(2)}) copy-start(f32[768]{0:T(1024)} %param.28) | copy-start | bytes 9220
  125.8 51.8 %copy-start.45 = (f32[3072]{0:T(1024)S(1)}, f32[3072]{0:T(1024)}, u32[]{:S(2)}) copy-start(f32[3072]{0:T(1024)} %param.30) | copy-start | bytes 36868
  125.8 147.5 %all-gather.5.cloned.1.call-start = ((), (), s32[]{:S(2)}) async-start(), calls=%async_computation.4 | async-start | bytes 5898240 | tf_op jit(solution)/shard_map/all_gather | solution.py:160
  175.7 57.2 %copy-start.23 = (f32[2,384]{1,0:T(2,128)}, f32[2,384]{1,0:T(2,128)S(1)}, u32[]{:S(2)}) copy-start(f32[2,384]{1,0:T(2,128)S(1)} %broadcast_multiply_fusion) | copy-start | bytes 9220
  177.7 55.3 %copy-start.27 = (f32[2,384]{1,0:T(2,128)}, f32[2,384]{1,0:T(2,128)S(1)}, u32[]{:S(2)}) copy-start(f32[2,384]{1,0:T(2,128)S(1)} %fusion.183) | copy-start | bytes 9220
  186.8 23.4 %copy-start.15 = (bf16[2,384,768]{2,1,0:T(8,128)(2,1)S(1)}, bf16[2,384,768]{2,1,0:T(8,128)(2,1)}, u32[]{:S(2)}) copy-start(bf16[2,384,768]{2,1,0:T(8,128)(2,1)} %param.33) | copy-start | bytes 3538948
  232.9 40.4 %copy-start.29 = (bf16[192,768]{1,0:T(8,128)(2,1)S(1)}, bf16[192,768]{1,0:T(8,128)(2,1)}, u32[]{:S(2)}) copy-start(bf16[192,768]{1,0:T(8,128)(2,1)} %param.25) | copy-start | bytes 884740
  232.9 45.4 %copy-start.39 = (f32[2,384]{1,0:T(2,128)}, f32[2,384]{1,0:T(2,128)S(1)}, u32[]{:S(2)}) copy-start(f32[2,384]{1,0:T(2,128)S(1)} %negate_multiply_fusion.2) | copy-start | bytes 9220
  235.7 388.1 %all-reduce.8.cloned.1.call-start = ((), (), s32[]{:S(2)}) async-start(), calls=%async_computation.7 | async-start | bytes 2359296 | tf_op jit(solution)/shard_map/psum | solution.py:177
  281.7 4.9 copy-start.12
  291.7 7.7 copy-start.4
  389.9 14.2 %copy-start.13 = (bf16[3,64,512]{2,1,0:T(8,128)(2,1)S(1)}, bf16[3,64,512]{2,1,0:T(8,128)(2,1)}, u32[]{:S(2)}) copy-start(bf16[3,64,512]{2,1,0:T(8,128)(2,1)} %fusion.377) | copy-start | bytes 589828 | tf_op jit(solution)/shard_map/while
  389.9 14.2 %copy-start.14 = (bf16[3,64,512]{2,1,0:T(8,128)(2,1)S(1)}, bf16[3,64,512]{2,1,0:T(8,128)(2,1)}, u32[]{:S(2)}) copy-start(bf16[3,64,512]{2,1,0:T(8,128)(2,1)} %fusion.378) | copy-start | bytes 589828 | tf_op jit(solution)/shard_map/while
  408.6 4.9 copy-start.12
  418.6 7.7 copy-start.4
  516.7 14.2 %copy-start.13 = (bf16[3,64,512]{2,1,0:T(8,128)(2,1)S(1)}, bf16[3,64,512]{2,1,0:T(8,128)(2,1)}, u32[]{:S(2)}) copy-start(bf16[3,64,512]{2,1,0:T(8,128)(2,1)} %fusion.377) | copy-start | bytes 589828 | tf_op jit(solution)/shard_map/while
  516.8 14.2 %copy-start.14 = (bf16[3,64,512]{2,1,0:T(8,128)(2,1)S(1)}, bf16[3,64,512]{2,1,0:T(8,128)(2,1)}, u32[]{:S(2)}) copy-start(bf16[3,64,512]{2,1,0:T(8,128)(2,1)} %fusion.378) | copy-start | bytes 589828 | tf_op jit(solution)/shard_map/while
  543.3 130.0 %reduce-scatter.5.cloned.1.call-start = ((), (), s32[]{:S(2)}) async-start(), calls=%async_computation.5 | async-start | bytes 5898240 | tf_op jit(solution)/shard_map/reduce_scatter | solution.py:171
  551.1 435.4 %all-reduce.6.cloned.1.call-start = ((), (), s32[]{:S(2)}) async-start(), calls=%async_computation.6 | async-start | bytes 37748736 | tf_op jit(solution)/shard_map/psum | solution.py:181
  551.1 10.6 %copy-start.6 = (bf16[2,384,768]{2,1,0:T(8,128)(2,1)S(1)}, bf16[2,384,768]{2,1,0:T(8,128)(2,1)}, u32[]{:S(2)}) copy-start(bf16[2,384,768]{2,1,0:T(8,128)(2,1)} %param.19) | copy-start | bytes 3538948
  551.1 10.6 %copy-start.8 = (bf16[2,384,768]{2,1,0:T(8,128)(2,1)S(1)}, bf16[2,384,768]{2,1,0:T(8,128)(2,1)}, u32[]{:S(2)}) copy-start(bf16[2,384,768]{2,1,0:T(8,128)(2,1)} %reduce-scatter.3.cloned.1.call-done) | copy-start | bytes 3538948
  551.2 10.5 %copy-start.22 = (f32[768]{0:T(1024)S(1)}, f32[768]{0:T(1024)}, u32[]{:S(2)}) copy-start(f32[768]{0:T(1024)} %param.26) | copy-start | bytes 9220
  551.2 10.5 %copy-start.24 = (f32[2,384]{1,0:T(2,128)S(1)}, f32[2,384]{1,0:T(2,128)}, u32[]{:S(2)}) copy-start(f32[2,384]{1,0:T(2,128)} %copy-done.23) | copy-start | bytes 9220
  551.2 10.5 %copy-start.26 = (f32[768]{0:T(1024)S(1)}, f32[768]{0:T(1024)}, u32[]{:S(2)}) copy-start(f32[768]{0:T(1024)} %param.27) | copy-start | bytes 9220
  551.2 10.5 %copy-start.28 = (f32[2,384]{1,0:T(2,128)S(1)}, f32[2,384]{1,0:T(2,128)}, u32[]{:S(2)}) copy-start(f32[2,384]{1,0:T(2,128)} %copy-done.27) | copy-start | bytes 9220
  551.2 10.5 %copy-start.31 = (f32[768]{0:T(1024)S(1)}, f32[768]{0:T(1024)}, u32[]{:S(2)}) copy-start(f32[768]{0:T(1024)} %param.28) | copy-start | bytes 9220
  571.7 8.8 copy-start.19
  580.5 92.9 %copy-start.33 = (f32[2,384]{1,0:T(2,128)S(1)}, f32[2,384]{1,0:T(2,128)}, u32[]{:S(2)}) copy-start(f32[2,384]{1,0:T(2,128)} %copy-done.32) | copy-start | bytes 9220
  580.5 92.9 %copy-start.34 = (f32[768]{0:T(1024)S(1)}, f32[768]{0:T(1024)}, u32[]{:S(2)}) copy-start(f32[768]{0:T(1024)} %param.21) | copy-start | bytes 9220
  580.5 95.1 %copy-start.42 = (f32[2,384]{1,0:T(2,128)S(1)}, f32[2,384]{1,0:T(2,128)}, u32[]{:S(2)}) copy-start(f32[2,384]{1,0:T(2,128)} %copy-done.41) | copy-start | bytes 9220
  580.5 95.1 %copy-start.38 = (f32[2,384]{1,0:T(2,128)S(1)}, f32[2,384]{1,0:T(2,128)}, u32[]{:S(2)}) copy-start(f32[2,384]{1,0:T(2,128)} %copy-done.37) | copy-start | bytes 9220
  580.9 97.5 %copy-start.36 = (f32[2,384]{1,0:T(2,128)S(1)}, f32[2,384]{1,0:T(2,128)}, u32[]{:S(2)}) copy-start(f32[2,384]{1,0:T(2,128)} %copy-done.35) | copy-start | bytes 9220
  580.9 97.5 %copy-start.40 = (f32[2,384]{1,0:T(2,128)S(1)}, f32[2,384]{1,0:T(2,128)}, u32[]{:S(2)}) copy-start(f32[2,384]{1,0:T(2,128)} %copy-done.39) | copy-start | bytes 9220
  673.3 5.1 copy-start.10
  673.3 5.1 copy-start.11
  673.3 5.1 copy-start.16
  986.5 8.8 slice-start
  986.5 8.8 slice-start.1
  986.5 8.8 slice-start.2
  (18 other events, 56.0 us)
Sparse Core Ops, SparseCore 0:
  14.7 40.1 all-gather.2
  126.0 47.8 reduce-scatter.2
  235.8 37.4 all-gather.4
  543.5 80.2 all-reduce.7
  626.2 47.1 reduce-scatter.4
  681.3 305.1 all-reduce.5
where the time goes:
time: 1010 us
  waiting for transfers between devices  454 us (45%)
  matrix products  354 us (35%)
  other arithmetic  75.9 us (8%)
  blocking collectives  64 us (6%)
  local copies, waits for them, and re-layouts  40.5 us (4%)
  between operations  14.8 us (1%)
    psum x1, waiting for transfers between devices, body(): lax.psum((grad_gain_one, grad_shift_one, grad_b_out, grad_gain_two, grad_...  263 us
    dot_general x6, matrix products, row_backward(): jnp.einsum('hqk,khe->qhe', score_grad, key_rows, preferred_element_type=j...  89.1 us
    dot_general x6, matrix products, row_backward(): jnp.einsum('hqk,qhe->khe', score_grad, query_block, preferred_element_typ...  87.3 us
    reduce_scatter x1, waiting for transfers between devices, body(): lax.psum_scatter(partial_out.astype(jnp.bfloat16), ('th', 'tw'), scatter_...  47.9 us
    reduce_scatter x1, waiting for transfers between devices, body(): lax.psum_scatter(grad_normed.astype(jnp.bfloat16), ('th', 'tw'), scatter_...  45.2 us
    psum x1, blocking collectives, body(): lax.psum((grad_gain_one, grad_shift_one, grad_b_out, grad_gain_two, grad_...  42.5 us
    all_gather x1, waiting for transfers between devices, body(): gathered = lax.all_gather(normed_low, ('th', 'tw'), axis=1, tiled=True)  40.1 us
    all_gather x1, waiting for transfers between devices, body(): grad_whole = lax.all_gather(grad_branch, ('th', 'tw'), axis=1, tiled=True)  37.6 us
  transfers between devices with their start and end apart: 6, of which 6 were waited for; matrix products, arithmetic and copies ran while one was open for 5% of the time, Pallas kernels for 0%

commit v1 on v0

--- a/solution.py
+++ b/solution.py
@@ -174,7 +174,7 @@
     grad_inputs, grad_gain_one, grad_shift_one = norm_one_back(grad_tile)
     grad_tokens = (grad_middle + grad_inputs).astype(jnp.bfloat16)
     head_sums = (
-        lax.psum(grad_w_qkv.astype(jnp.bfloat16), "dp").astype(jnp.float32),
+        jnp.sum(lax.all_gather(grad_w_qkv.astype(jnp.bfloat16), "dp"), axis=0).astype(jnp.float32),
         lax.psum(grad_b_qv.astype(jnp.bfloat16), "dp").astype(jnp.float32),
         lax.psum(grad_w_out.astype(jnp.bfloat16), "dp").astype(jnp.float32),
     )

time: 1010 us -> 1100 us (1.089)
  waiting for transfers between devices: 454 us -> 544 us
    all_gather x0 -> x1, waiting for transfers between devices: none -> 61.8 us  [body(): lax.all_gather(grad_w_qkv.astype(jnp.bfloat16), 'dp')]
    psum x1, waiting for transfers between devices: 263 us -> 305 us  [body(): lax.psum((grad_gain_one, grad_shift_one, grad_b_out, grad_gain_two, grad_...]
    psum x1, waiting for transfers between devices: 20.8 us -> 4.2 us  [body(): lax.psum(grad_w_out.astype(jnp.bfloat16), 'dp').astype(jnp.float32)]
  transfers between devices with their start and end apart: 6 -> 7, of which waited for: 6 -> 7; matrix products, arithmetic and copies ran while one was open for 5% -> 5% of each run, Pallas kernels for 0% -> 0%
where the time goes in v1:
time: 1100 us
  waiting for transfers between devices  544 us (49%)
  matrix products  356 us (32%)
  other arithmetic  79 us (7%)
  blocking collectives  64.1 us (6%)
  local copies, waits for them, and re-layouts  40.5 us (4%)
  between operations  14.8 us (1%)
    psum x1, waiting for transfers between devices, body(): lax.psum((grad_gain_one, grad_shift_one, grad_b_out, grad_gain_two, grad_...  305 us
    dot_general x6, matrix products, row_backward(): jnp.einsum('hqk,khe->qhe', score_grad, key_rows, preferred_element_type=j...  89.4 us
    dot_general x6, matrix products, row_backward(): jnp.einsum('hqk,qhe->khe', score_grad, query_block, preferred_element_typ...  87.3 us
    all_gather x1, waiting for transfers between devices, body(): lax.all_gather(grad_w_qkv.astype(jnp.bfloat16), 'dp')  61.8 us
    reduce_scatter x1, waiting for transfers between devices, body(): lax.psum_scatter(partial_out.astype(jnp.bfloat16), ('th', 'tw'), scatter_...  47.9 us
    reduce_scatter x1, waiting for transfers between devices, body(): lax.psum_scatter(grad_normed.astype(jnp.bfloat16), ('th', 'tw'), scatter_...  47.5 us
    psum x1, blocking collectives, body(): lax.psum((grad_gain_one, grad_shift_one, grad_b_out, grad_gain_two, grad_...  42.8 us
    all_gather x1, waiting for transfers between devices, body(): gathered = lax.all_gather(normed_low, ('th', 'tw'), axis=1, tiled=True)  40.1 us
  transfers between devices with their start and end apart: 7, of which 7 were waited for; matrix products, arithmetic and copies ran while one was open for 5% of the time, Pallas kernels for 0%

profile of v1, /device:TPU:0, one launch (start us, length us, event | category | flops | bytes accessed | tf_op | source)
XLA Modules:
  0.0 1100.8 jit_solution(15991996567226168997)
XLA Ops:
  14.8 40.1 %all-gather.5.cloned.1.call-done = bf16[2,1536,768]{2,1,0:T(8,128)(2,1)} async-done(((bf16[2,384,768]{2,1,0:T(8,128)(2,1)}), bf16[2,1536,768]{2,1,0:T(8,128)(2,1)}) %all-gather.5.cloned.1.call-update) | async-done | bytes 4718608 | tf_op jit(solution)/shard_map/all_gather | solution.py:119
  54.9 6.8 fusion.154
  61.6 59.3 %while.22 = (s32[]{:T(128)}, bf16[2,1536,192]{1,2,0:T(8,128)(2,1)S(1)}, f32[2,3,1536]{2,1,0:T(4,128)S(1)}, bf16[2,3,1536,192]{2,3,1,0:T(8,128)(2,1)}, s32[2,1536...) while((s32[]{:T(128)}, bf16[2,1536,192]{1,2,0:T(8,128)(2,1)S(1)}, ...), condition=%wide.region_9.10_spmd, body=%wide.region_2.9_spmd.sunk | while | flops 1901302272 | bytes 107581632 | solution.py:123
  78.8 5.2 fusion.324
  108.0 5.2 fusion.324
  120.9 4.9 convolution_convert_fusion
  126.0 47.9 %reduce-scatter.3.cloned.1.call-done = bf16[2,384,768]{2,1,0:T(8,128)(2,1)} async-done(((bf16[2,1536,768]{2,1,0:T(8,128)(2,1)}), bf16[2,384,768]{2,1,0:T(8,128)(2,1)}) %reduce-scatter.3.cloned.1.call-update) | async-done | bytes 1179664 | tf_op jit(solution)/shard_map/reduce_scatter | solution.py:126
  177.7 9.2 fusion.165
  186.9 23.4 %multiply_convert_fusion.3 = (bf16[2,384,3072]{2,1,0:T(8,128)(2,1)}, f32[2,384,3072]{2,1,0:T(8,128)}) fusion(f32[2,384,3072]{2,1,0:T(8,128)S(1)} %get-tuple-element.162, f32[3072]{0:T(1024)S(1)} %copy-done.44, u8[384,3072]{1,0:T(8,128)(4,1)S(1)} %get-tuple-element.78, u8[384,3072]{1,0:T(8,128)(4,1)S(1)} %get-tuple-element.77), kind=kLoop, calls=%fused_computation.126 | loop fusion | flops 167510016 | bytes 25964544 | tf_op jit(solution)/shard_map/convert_element_type | solution.py:138
  210.3 12.5 %convert_reduce_fusion = (f32[3072]{0:T(1024)}, bf16[2,384,3072]{2,1,0:T(8,128)(2,1)}) fusion(f32[2,384,3072]{2,1,0:T(8,128)} %get-tuple-element.121, bf16[2,384,768]{2,1,0:T(8,128)(2,1)S(1)} %copy-done.15, bf16[3072,768]{1,0:T(8,128)(2,1)} %param.31, f32[2,384,3072]{2,1,0:T(8,128)S(1)} %get-tuple-element.162, f32[3072]{0:T(1024)S(1)} %copy-done.44), kind=kOutput, calls=%fused_computation.124 | convolution fusion | flops 3663983616 | bytes 29515776 | tf_op jit(solution)/shard_map/rld,fd->rlf/dot_general | solution.py:147
  222.8 8.1 fusion.185
  235.8 37.6 %all-gather.7.cloned.1.call-done = bf16[2,1536,768]{2,1,0:T(8,128)(2,1)} async-done(((bf16[2,384,768]{2,1,0:T(8,128)(2,1)}), bf16[2,1536,768]{2,1,0:T(8,128)(2,1)}) %all-gather.7.cloned.1.call-update) | async-done | bytes 4718608 | tf_op jit(solution)/shard_map/all_gather | solution.py:160
  273.4 5.0 convolution_convert_fusion.1
  278.4 254.5 %while.23 = (s32[]{:T(128)}, bf16[2,3,1536,192]{2,3,1,0:T(8,128)(2,1)}, bf16[2,3,1536,192]{2,3,1,0:T(8,128)(2,1)}, s32[2,1536]{1,0:T(2,128)S(1)}, f32[2,3,1536]{...) while((s32[]{:T(128)}, ...), condition=%wide.region_19.20_spmd, body=%wide.region_15.19_spmd.sunk | while | flops 4682926080 | bytes 364640672 | solution.py:167
  294.3 4.3 copy-done.3
  300.5 5.2 fusion.371
  305.6 15.2 %fusion.377 = bf16[3,64,512]{2,1,0:T(8,128)(2,1)} fusion(bf16[1536,3,64]{0,2,1:T(8,128)(2,1)S(1)} %bitcast.313, f32[3,512,1536]{2,1,0:T(8,128)} %copy-done.4, f32[3,512,1536]{2,1,0:T(8,128)} %fusion.371), kind=kOutput, calls=%fused_computation.94.clone.1 | convolution fusion | flops 320965632 | bytes 19660800 | tf_op jit(solution)/shard_map/while/body/eval_jaxpr/hqk,khe->qhe/dot_general | solution.py:82
  320.8 15.3 %fusion.372 = f32[3,64,1536]{2,1,0:T(8,128)} fusion(bf16[512,3,64]{0,2,1:T(8,128)(2,1)} %bitcast.325, f32[3,512,1536]{2,1,0:T(8,128)} %copy-done.4, f32[3,512,1536]{2,1,0:T(8,128)} %fusion.371), kind=kOutput, calls=%fused_computation.63.clone.1 | convolution fusion | flops 320867328 | bytes 20250624 | tf_op jit(solution)/shard_map/while/body/eval_jaxpr/hqk,qhe->khe/dot_general | solution.py:86
  336.2 5.2 fusion.375
  341.3 14.3 %fusion.379 = bf16[3,64,512]{2,1,0:T(8,128)(2,1)S(1)} fusion(bf16[1536,3,64]{0,2,1:T(8,128)(2,1)S(1)} %bitcast.314, f32[3,512,1536]{2,1,0:T(8,128)} %copy-done.3, f32[3,512,1536]{2,1,0:T(8,128)} %fusion.375), kind=kOutput, calls=%fused_computation.92.clone.1 | convolution fusion | flops 320965632 | bytes 19660800 | tf_op jit(solution)/shard_map/while/body/eval_jaxpr/hqk,khe->qhe/dot_general | solution.py:82
  355.7 5.2 fusion.373
  360.8 15.2 %fusion.378 = bf16[3,64,512]{2,1,0:T(8,128)(2,1)} fusion(bf16[1536,3,64]{0,2,1:T(8,128)(2,1)S(1)} %bitcast.315, f32[3,512,1536]{2,1,0:T(8,128)} %copy-done.2, f32[3,512,1536]{2,1,0:T(8,128)} %fusion.373), kind=kOutput, calls=%fused_computation.93.clone.1 | convolution fusion | flops 320965632 | bytes 19660800 | tf_op jit(solution)/shard_map/while/body/eval_jaxpr/hqk,khe->qhe/dot_general | solution.py:82
  376.0 14.3 %fusion.374 = f32[3,64,1536]{2,1,0:T(8,128)} fusion(bf16[512,3,64]{0,2,1:T(8,128)(2,1)S(1)} %bitcast.323, f32[3,512,1536]{2,1,0:T(8,128)} %copy-done.2, f32[3,512,1536]{2,1,0:T(8,128)} %fusion.373), kind=kOutput, calls=%fused_computation.67.clone.1 | convolution fusion | flops 320867328 | bytes 20250624 | tf_op jit(solution)/shard_map/while/body/eval_jaxpr/hqk,qhe->khe/dot_general | solution.py:86
  390.4 13.9 %fusion.376 = bf16[3,64,1536]{2,1,0:T(8,128)(2,1)S(1)} fusion(f32[3,64,1536]{2,1,0:T(8,128)} %fusion.372, f32[3,64,1536]{2,1,0:T(8,128)} %fusion.374, bf16[512,3,64]{0,2,1:T(8,128)(2,1)S(1)} %bitcast.321, f32[3,512,1536]{2,1,0:T(8,128)} %copy-done.3, f32[3,512,1536]{2,1,0:T(8,128)} %fusion.375), kind=kOutput, calls=%fused_computation.79.clone.1 | convolution fusion | flops 321752064 | bytes 22020096 | tf_op jit(solution)/shard_map/while/body/eval_jaxpr/hqk,qhe->khe/dot_general | solution.py:86
  421.3 4.3 copy-done.3
  427.5 5.2 fusion.371
  432.6 15.2 %fusion.377 = bf16[3,64,512]{2,1,0:T(8,128)(2,1)} fusion(bf16[1536,3,64]{0,2,1:T(8,128)(2,1)S(1)} %bitcast.313, f32[3,512,1536]{2,1,0:T(8,128)} %copy-done.4, f32[3,512,1536]{2,1,0:T(8,128)} %fusion.371), kind=kOutput, calls=%fused_computation.94.clone.1 | convolution fusion | flops 320965632 | bytes 19660800 | tf_op jit(solution)/shard_map/while/body/eval_jaxpr/hqk,khe->qhe/dot_general | solution.py:82
  447.8 15.3 %fusion.372 = f32[3,64,1536]{2,1,0:T(8,128)} fusion(bf16[512,3,64]{0,2,1:T(8,128)(2,1)} %bitcast.325, f32[3,512,1536]{2,1,0:T(8,128)} %copy-done.4, f32[3,512,1536]{2,1,0:T(8,128)} %fusion.371), kind=kOutput, calls=%fused_computation.63.clone.1 | convolution fusion | flops 320867328 | bytes 20250624 | tf_op jit(solution)/shard_map/while/body/eval_jaxpr/hqk,qhe->khe/dot_general | solution.py:86
  463.2 5.2 fusion.375
  468.3 14.3 %fusion.379 = bf16[3,64,512]{2,1,0:T(8,128)(2,1)S(1)} fusion(bf16[1536,3,64]{0,2,1:T(8,128)(2,1)S(1)} %bitcast.314, f32[3,512,1536]{2,1,0:T(8,128)} %copy-done.3, f32[3,512,1536]{2,1,0:T(8,128)} %fusion.375), kind=kOutput, calls=%fused_computation.92.clone.1 | convolution fusion | flops 320965632 | bytes 19660800 | tf_op jit(solution)/shard_map/while/body/eval_jaxpr/hqk,khe->qhe/dot_general | solution.py:82
  482.7 5.2 fusion.373
  487.8 15.2 %fusion.378 = bf16[3,64,512]{2,1,0:T(8,128)(2,1)} fusion(bf16[1536,3,64]{0,2,1:T(8,128)(2,1)S(1)} %bitcast.315, f32[3,512,1536]{2,1,0:T(8,128)} %copy-done.2, f32[3,512,1536]{2,1,0:T(8,128)} %fusion.373), kind=kOutput, calls=%fused_computation.93.clone.1 | convolution fusion | flops 320965632 | bytes 19660800 | tf_op jit(solution)/shard_map/while/body/eval_jaxpr/hqk,khe->qhe/dot_general | solution.py:82
  503.0 14.3 %fusion.374 = f32[3,64,1536]{2,1,0:T(8,128)} fusion(bf16[512,3,64]{0,2,1:T(8,128)(2,1)S(1)} %bitcast.323, f32[3,512,1536]{2,1,0:T(8,128)} %copy-done.2, f32[3,512,1536]{2,1,0:T(8,128)} %fusion.373), kind=kOutput, calls=%fused_computation.67.clone.1 | convolution fusion | flops 320867328 | bytes 20250624 | tf_op jit(solution)/shard_map/while/body/eval_jaxpr/hqk,qhe->khe/dot_general | solution.py:86
  517.4 13.9 %fusion.376 = bf16[3,64,1536]{2,1,0:T(8,128)(2,1)S(1)} fusion(f32[3,64,1536]{2,1,0:T(8,128)} %fusion.372, f32[3,64,1536]{2,1,0:T(8,128)} %fusion.374, bf16[512,3,64]{0,2,1:T(8,128)(2,1)S(1)} %bitcast.321, f32[3,512,1536]{2,1,0:T(8,128)} %copy-done.3, f32[3,512,1536]{2,1,0:T(8,128)} %fusion.375), kind=kOutput, calls=%fused_computation.79.clone.1 | convolution fusion | flops 321752064 | bytes 22020096 | tf_op jit(solution)/shard_map/while/body/eval_jaxpr/hqk,qhe->khe/dot_general | solution.py:86
  532.9 4.5 fusion.177
  537.5 7.7 bitcast_convert_fusion
  545.3 7.2 fusion.174
  552.7 10.5 convolution_bitcast_fusion
  563.2 9.2 convolution_bitcast_fusion.1
  573.2 8.8 add_convert_fusion.3
  582.4 21.3 %psum.79 = bf16[2,192]{1,0:T(2,128)(2,1)S(1)} all-reduce(bf16[2,192]{1,0:T(2,128)(2,1)S(1)} %slice_reduce_fusion), channel_id=1, replica_groups=mesh['dp'=8,'th'=2,'tw'=2] {'dp'}, use_global_device_ids=true, to_apply=%region_29.30 | all-reduce | flops 384 | bytes 1536 | tf_op jit(solution)/shard_map/psum | solution.py:178
  604.3 4.2 all-reduce.5.cloned.1.call-done
  610.3 47.5 %reduce-scatter.5.cloned.1.call-done = bf16[2,384,768]{2,1,0:T(8,128)(2,1)} async-done(((bf16[2,1536,768]{2,1,0:T(8,128)(2,1)}), bf16[2,384,768]{2,1,0:T(8,128)(2,1)}) %reduce-scatter.5.cloned.1.call-update) | async-done | bytes 1179664 | tf_op jit(solution)/shard_map/reduce_scatter | solution.py:171
  666.0 42.8 %all-reduce = (f32[768]{0:T(1024)}, f32[768]{0:T(1024)}, f32[768]{0:T(1024)}, f32[768]{0:T(1024)}, f32[768]{0:T(1024)}, /*index=5*/f32[3072]{0:T(1024)}, f32[768]{0:T(1024)}) all-reduce(f32[768]{0:T(1024)S(1)} %get-tuple-element.81, f32[768]{0:T(1024)S(1)} %get-tuple-element.85, ...), channel_id=1, replica_groups=mesh['dp'=8,'th'=2,'tw'=2] {'dp','th','tw'}, use_global_device_ids=true, to_apply=%region_24.25 | all-reduce | flops 7680 | bytes 61440 | tf_op jit(solution)/shard_map/psum | solution.py:181
  708.8 61.8 %all-gather.9.cloned.1.call-done = bf16[24,768,192]{1,2,0:T(8,128)(2,1)} async-done(((bf16[3,768,192]{1,2,0:T(8,128)(2,1)}), bf16[24,768,192]{1,2,0:T(8,128)(2,1)}) %all-gather.9.cloned.1.call-update) | async-done | bytes 7077904 | tf_op jit(solution)/shard_map/all_gather | solution.py:177
  770.6 4.2 reduce_sum.255
  776.1 305.1 %all-reduce.7.cloned.1.call-done = (f32[768,3072]{1,0:T(8,128)}, f32[3072,768]{1,0:T(8,128)}) async-done(((f32[768,3072]{1,0:T(8,128)}, f32[3072,768]{1,0:T(8,128)}), (f32[768,3072]{1,0:T(8,128)}, f32[3072,768]{1,0:T(8,128)})) %all-reduce.7.cloned.1.call-update) | async-done | bytes 18874384 | tf_op jit(solution)/shard_map/psum | solution.py:181
  1081.2 8.8 copy.61
  (230 shorter events, 118.3 us)
Async XLA Ops:
  7.2 47.7 %copy-start = (bf16[3,768,192]{1,2,0:T(8,128)(2,1)S(1)}, bf16[3,768,192]{1,2,0:T(8,128)(2,1)}, u32[]{:S(2)}) copy-start(bf16[3,768,192]{1,2,0:T(8,128)(2,1)} %param.23) | copy-start | bytes 2654212
  7.2 7.5 copy-start.47
  7.2 47.7 %all-gather.5.cloned.1.call-start = ((), (), s32[]{:S(2)}) async-start(), calls=%async_computation.2 | async-start | bytes 5898240 | tf_op jit(solution)/shard_map/all_gather | solution.py:119
  14.6 159.3 %reduce-scatter.3.cloned.1.call-start = ((), (), s32[]{:S(2)}) async-start(), calls=%async_computation.3 | async-start | bytes 5898240 | tf_op jit(solution)/shard_map/reduce_scatter | solution.py:126
  14.8 46.8 %copy-start.19 = (s32[2,1536]{1,0:T(2,128)S(1)}, s32[2,1536]{1,0:T(2,128)}, u32[]{:S(2)}) copy-start(s32[2,1536]{1,0:T(2,128)} %param.20) | copy-start | bytes 36868
  120.9 5.0 copy-start.17
  120.9 53.0 %copy-start.5 = (bf16[2,384,768]{2,1,0:T(8,128)(2,1)S(1)}, bf16[2,384,768]{2,1,0:T(8,128)(2,1)}, u32[]{:S(2)}) copy-start(bf16[2,384,768]{2,1,0:T(8,128)(2,1)} %param.19) | copy-start | bytes 3538948
  120.9 53.0 %copy-start.20 = (f32[768]{0:T(1024)S(1)}, f32[768]{0:T(1024)}, u32[]{:S(2)}) copy-start(f32[768]{0:T(1024)} %param.26) | copy-start | bytes 9220
  125.9 51.8 %copy-start.24 = (f32[768]{0:T(1024)S(1)}, f32[768]{0:T(1024)}, u32[]{:S(2)}) copy-start(f32[768]{0:T(1024)} %param.27) | copy-start | bytes 9220
  125.9 51.8 %copy-start.29 = (f32[768]{0:T(1024)S(1)}, f32[768]{0:T(1024)}, u32[]{:S(2)}) copy-start(f32[768]{0:T(1024)} %param.28) | copy-start | bytes 9220
  125.9 51.8 %copy-start.44 = (f32[3072]{0:T(1024)S(1)}, f32[3072]{0:T(1024)}, u32[]{:S(2)}) copy-start(f32[3072]{0:T(1024)} %param.30) | copy-start | bytes 36868
  125.9 147.4 %all-gather.7.cloned.1.call-start = ((), (), s32[]{:S(2)}) async-start(), calls=%async_computation.4 | async-start | bytes 5898240 | tf_op jit(solution)/shard_map/all_gather | solution.py:160
  175.7 57.2 %copy-start.22 = (f32[2,384]{1,0:T(2,128)}, f32[2,384]{1,0:T(2,128)S(1)}, u32[]{:S(2)}) copy-start(f32[2,384]{1,0:T(2,128)S(1)} %broadcast_multiply_fusion) | copy-start | bytes 9220
  177.7 55.3 %copy-start.26 = (f32[2,384]{1,0:T(2,128)}, f32[2,384]{1,0:T(2,128)S(1)}, u32[]{:S(2)}) copy-start(f32[2,384]{1,0:T(2,128)S(1)} %fusion.183) | copy-start | bytes 9220
  186.9 23.4 %copy-start.15 = (bf16[2,384,768]{2,1,0:T(8,128)(2,1)S(1)}, bf16[2,384,768]{2,1,0:T(8,128)(2,1)}, u32[]{:S(2)}) copy-start(bf16[2,384,768]{2,1,0:T(8,128)(2,1)} %param.33) | copy-start | bytes 3538948
  233.0 40.4 %copy-start.28 = (bf16[192,768]{1,0:T(8,128)(2,1)S(1)}, bf16[192,768]{1,0:T(8,128)(2,1)}, u32[]{:S(2)}) copy-start(bf16[192,768]{1,0:T(8,128)(2,1)} %param.25) | copy-start | bytes 884740
  233.0 45.4 %copy-start.38 = (f32[2,384]{1,0:T(2,128)}, f32[2,384]{1,0:T(2,128)S(1)}, u32[]{:S(2)}) copy-start(f32[2,384]{1,0:T(2,128)S(1)} %negate_multiply_fusion.2) | copy-start | bytes 9220
  235.7 372.8 %all-reduce.5.cloned.1.call-start = ((), (), s32[]{:S(2)}) async-start(), calls=%async_computation.6 | async-start | bytes 589824 | tf_op jit(solution)/shard_map/psum | solution.py:179
  281.8 4.9 copy-start.12
  291.8 7.7 copy-start.4
  390.4 14.0 %copy-start.13 = (bf16[3,64,512]{2,1,0:T(8,128)(2,1)S(1)}, bf16[3,64,512]{2,1,0:T(8,128)(2,1)}, u32[]{:S(2)}) copy-start(bf16[3,64,512]{2,1,0:T(8,128)(2,1)} %fusion.377) | copy-start | bytes 589828 | tf_op jit(solution)/shard_map/while
  390.4 14.0 %copy-start.14 = (bf16[3,64,512]{2,1,0:T(8,128)(2,1)S(1)}, bf16[3,64,512]{2,1,0:T(8,128)(2,1)}, u32[]{:S(2)}) copy-start(bf16[3,64,512]{2,1,0:T(8,128)(2,1)} %fusion.378) | copy-start | bytes 589828 | tf_op jit(solution)/shard_map/while
  418.8 7.7 copy-start.4
  517.4 14.0 %copy-start.13 = (bf16[3,64,512]{2,1,0:T(8,128)(2,1)S(1)}, bf16[3,64,512]{2,1,0:T(8,128)(2,1)}, u32[]{:S(2)}) copy-start(bf16[3,64,512]{2,1,0:T(8,128)(2,1)} %fusion.377) | copy-start | bytes 589828 | tf_op jit(solution)/shard_map/while
  517.4 14.0 %copy-start.14 = (bf16[3,64,512]{2,1,0:T(8,128)(2,1)S(1)}, bf16[3,64,512]{2,1,0:T(8,128)(2,1)}, u32[]{:S(2)}) copy-start(bf16[3,64,512]{2,1,0:T(8,128)(2,1)} %fusion.378) | copy-start | bytes 589828 | tf_op jit(solution)/shard_map/while
  537.4 120.4 %reduce-scatter.5.cloned.1.call-start = ((), (), s32[]{:S(2)}) async-start(), calls=%async_computation.5 | async-start | bytes 5898240 | tf_op jit(solution)/shard_map/reduce_scatter | solution.py:171
  545.2 225.4 %all-gather.9.cloned.1.call-start = ((), (), s32[]{:S(2)}) async-start(), calls=%async_computation.7 | async-start | bytes 7962624 | tf_op jit(solution)/shard_map/all_gather | solution.py:177
  552.6 528.7 %all-reduce.7.cloned.1.call-start = ((), (), s32[]{:S(2)}) async-start(), calls=%async_computation.8 | async-start | bytes 37748736 | tf_op jit(solution)/shard_map/psum | solution.py:181
  552.6 10.6 copy-start.6
  552.6 10.6 copy-start.8
  552.6 10.6 copy-start.21
  552.6 10.6 copy-start.23
  552.6 10.6 copy-start.25
  552.7 10.6 copy-start.27
  552.7 10.6 copy-start.30
  573.2 8.8 copy-start.18
  573.2 84.7 %copy-start.32 = (f32[2,384]{1,0:T(2,128)S(1)}, f32[2,384]{1,0:T(2,128)}, u32[]{:S(2)}) copy-start(f32[2,384]{1,0:T(2,128)} %copy-done.31) | copy-start | bytes 9220
  573.2 84.7 %copy-start.33 = (f32[768]{0:T(1024)S(1)}, f32[768]{0:T(1024)}, u32[]{:S(2)}) copy-start(f32[768]{0:T(1024)} %param.21) | copy-start | bytes 9220
  582.0 78.2 %copy-start.41 = (f32[2,384]{1,0:T(2,128)S(1)}, f32[2,384]{1,0:T(2,128)}, u32[]{:S(2)}) copy-start(f32[2,384]{1,0:T(2,128)} %copy-done.40) | copy-start | bytes 9220
  582.0 78.2 %copy-start.37 = (f32[2,384]{1,0:T(2,128)S(1)}, f32[2,384]{1,0:T(2,128)}, u32[]{:S(2)}) copy-start(f32[2,384]{1,0:T(2,128)} %copy-done.36) | copy-start | bytes 9220
  582.0 80.9 %copy-start.35 = (f32[2,384]{1,0:T(2,128)S(1)}, f32[2,384]{1,0:T(2,128)}, u32[]{:S(2)}) copy-start(f32[2,384]{1,0:T(2,128)} %copy-done.34) | copy-start | bytes 9220
  582.0 80.9 %copy-start.39 = (f32[2,384]{1,0:T(2,128)S(1)}, f32[2,384]{1,0:T(2,128)}, u32[]{:S(2)}) copy-start(f32[2,384]{1,0:T(2,128)} %copy-done.38) | copy-start | bytes 9220
  657.9 5.1 copy-start.10
  657.9 5.1 copy-start.11
  657.9 5.1 copy-start.16
  1081.2 8.8 slice-start
  1081.2 8.8 slice-start.1
  1081.2 8.8 slice-start.2
  (18 other events, 56.3 us)
Sparse Core Ops, SparseCore 0:
  14.7 40.1 all-gather.4
  126.0 47.8 reduce-scatter.2
  235.9 37.4 all-gather.6
  537.6 70.9 all-reduce.4
  610.9 46.9 reduce-scatter.4
  660.7 109.8 all-gather.8
  778.7 302.4 all-reduce.6
